TPU v7x, 128 devices: a whole 4x4x4 slice. The times are simulated.
128 devices in a mesh: row: 8 (over z, x_hi), col: 16 (over x_lo, y, core).
Axes of the slice: x: 4 (x_hi: 2, x_lo: 2; x = x_hi * 2 + x_lo), y: 4, z: 4, core: 2. Of those that a mesh axis runs over, the one named last changes fastest.
Arguments:
- factor: float32 [16384, 16384], P(('row', 'col')), as said below
- damping: float32 [16384], P(('row', 'col')), may hold values from 0.1 to 1
- gradients: float32 [3072, 128], replicated, may hold values from -6 to 6
- inverses: float32 [5, 512, 512], replicated, as said below
Outputs:
- updated: float32 [8, 8, 256, 4, 16, 256], P(None, 'row', None, None, 'col')
- panel_tiles: float32 [8, 8, 256, 512], P(None, 'row', 'col')
- solution: float32 [3072, 128], replicated
Inputs may be any that keep to these rules, and one draw needn't show every extreme that they name: `factor`: symmetric. `inverses`: one matrix for each diagonal block after the first.
All inputs are finite; a program needn't handle non-finite values.
Results may differ from a plain program's by a relative error of at most 0.0001.
Values sent between devices are 32-bit elements; how exact they have to be, the bound alone decides.
No kernel may reach another device: no remote copies, remote signals or barrier semaphores. Data moves between devices by JAX's collectives and lax.ppermute only.
A program may use at most 128 MiB of HBM per device.

v0:
```python
import jax
import jax.numpy as jnp
from jax import lax
from jax.sharding import PartitionSpec as P


def spread_2(block, axis, source):
    block = jnp.where(lax.axis_index(axis) == source, block, jnp.zeros_like(block))
    return lax.psum(block, axis)


def right_solve(corner_factor, panel_rows):
    return jax.scipy.linalg.solve_triangular(corner_factor, panel_rows.T, lower=True).T


def exact_dot(left, right):
    return jnp.dot(left, right, precision=lax.Precision.HIGHEST, preferred_element_type=jnp.float32)


def locate(block_index, position, axis_count, tile_size, block_width):
    piece_width = min(tile_size, block_width)
    pieces = block_width // piece_width
    first_tile = block_index * block_width // tile_size
    offset = block_index * block_width % tile_size
    turn_index = (position - first_tile) % axis_count
    is_valid = turn_index < pieces
    local_start = (first_tile + turn_index) // axis_count * tile_size + offset
    return (local_start, turn_index * piece_width, is_valid)


def place(segment, place_at, block_width, axis_dim):
    extent = list(segment.shape)
    extent[axis_dim] = block_width + segment.shape[axis_dim]
    buffer = jnp.zeros(tuple(extent), segment.dtype)
    filled = lax.dynamic_update_slice_in_dim(buffer, segment, place_at, axis_dim)
    return lax.slice_in_dim(filled, 0, block_width, axis=axis_dim)


def body(factor, damping, gradients, inverses):
    row_count = lax.axis_size("row")
    col_count = lax.axis_size("col")
    part_rows, order_size = factor.shape
    panel_width = inverses.shape[1]
    tile_size = order_size // (row_count * row_count)
    col_tiles = order_size // (col_count * tile_size)
    local_cols = col_tiles * tile_size
    local_rows = row_count * tile_size
    piece_width = min(tile_size, panel_width)
    share_rows = tile_size // col_count
    lead_share = panel_width // col_count
    row_index = lax.axis_index("row")
    col_index = lax.axis_index("col")
    first_col = (row_index * col_count + col_index) * part_rows
    square = lax.dynamic_slice_in_dim(factor, first_col, part_rows, 1) + jnp.diag(damping)
    damped = lax.dynamic_update_slice_in_dim(factor, square, first_col, 1)
    arranged = damped.reshape(part_rows, col_tiles, col_count, tile_size).transpose(2, 0, 1, 3)
    arranged = arranged.reshape(col_count, part_rows, local_cols)
    carried = None
    spread = lax.all_to_all(arranged, "col", split_axis=0, concat_axis=1, tiled=True)
    landed = lax.all_to_all(spread, "row", split_axis=1, concat_axis=0, tiled=True)
    local_block = landed.reshape(local_rows, local_cols)
    row_start, row_place, row_valid = locate(0, row_index, row_count, tile_size, panel_width)
    col_start, col_place, col_valid = locate(0, col_index, col_count, tile_size, panel_width)
    col_piece = lax.dynamic_slice_in_dim(local_block, col_start, piece_width, 1) * col_valid.astype(
        jnp.float32
    )
    contrib = place(col_piece, col_place, panel_width, 1)
    corner_piece = lax.dynamic_slice_in_dim(contrib, row_start, piece_width, 0) * row_valid.astype(
        jnp.float32
    )
    corner = lax.psum(place(corner_piece, row_place, panel_width, 0), ("row", "col"))
    corner_factor = jnp.linalg.cholesky(corner)
    panel_rows = lax.psum(contrib, "col")
    factor_rows = right_solve(corner_factor, panel_rows)
    own_factor = lax.dynamic_slice_in_dim(
        factor_rows.reshape(row_count, tile_size, panel_width),
        col_index * share_rows,
        share_rows,
        1,
    )
    grouped = factor_rows.reshape(col_tiles, col_count // row_count, tile_size, panel_width)
    picked = lax.dynamic_index_in_dim(grouped, col_index // row_count, 1, keepdims=False)
    picked = picked.reshape(local_cols, panel_width)
    factor_cols = spread_2(picked, "row", col_index % row_count)
    outer_part = lax.dot_general(
        factor_rows,
        factor_cols,
        (((1,), (1,)), ((), ())),
        precision=lax.Precision.HIGHEST,
        preferred_element_type=jnp.float32,
    )
    trailing = local_block - outer_part
    block_count = gradients.shape[0] // panel_width
    first_block = jax.scipy.linalg.solve_triangular(
        corner_factor, gradients[:panel_width], lower=True
    )
    solved = [first_block]
    known_cols = jnp.zeros((local_cols, gradients.shape[1]), jnp.float32)
    lead_start = col_index * lead_share
    first_share = lax.dynamic_slice_in_dim(first_block, lead_start, lead_share, 0)
    for block_index in range(1, block_count):
        if block_index > 1:
            put_start, put_place, put_valid = locate(
                block_index - 1, col_index, col_count, tile_size, panel_width
            )
            segment = lax.dynamic_slice_in_dim(solved[-1], put_place, piece_width, 0)
            current = lax.dynamic_slice_in_dim(known_cols, put_start, piece_width, 0)
            known_cols = lax.dynamic_update_slice_in_dim(
                known_cols, jnp.where(put_valid, segment, current), put_start, 0
            )
        block_start, block_place, block_valid = locate(
            block_index, row_index, row_count, tile_size, panel_width
        )
        lead_rows = lax.dynamic_slice_in_dim(factor_rows, block_start, piece_width, 0)
        lead_part = lax.dynamic_slice_in_dim(lead_rows, lead_start, lead_share, 1)
        partial_value = exact_dot(lead_part, first_share)
        if block_index > 1:
            schur_rows = lax.dynamic_slice_in_dim(trailing, block_start, piece_width, 0)
            partial_value = partial_value + exact_dot(schur_rows, known_cols)
        partial_value = partial_value * block_valid.astype(jnp.float32)
        summed = lax.psum(place(partial_value, block_place, panel_width, 0), ("row", "col"))
        right_side = gradients[block_index * panel_width : (block_index + 1) * panel_width]
        solved.append(exact_dot(inverses[block_index - 1], right_side - summed))
    solution = jnp.concatenate(solved, axis=0)
    updated = trailing.reshape(row_count, 1, tile_size, col_tiles, 1, tile_size)
    panel_tiles = own_factor.reshape(row_count, 1, share_rows, panel_width)
    return (updated, panel_tiles, solution)


def solution(mesh):
    return jax.shard_map(
        body,
        mesh=mesh,
        in_specs=(P(("row", "col"), None), P(("row", "col")), P(), P()),
        out_specs=(P(None, "row", None, None, "col", None), P(None, "row", "col", None), P()),
        check_vma=False,
    )
```

profile of v0, /device:TPU:1, one launch (start us, length us, event | category | flops | bytes accessed | tf_op | source)
XLA Modules:
  0.0 1456.4 jit_solution(4369769002759106836)
XLA Ops:
  7.2 7.6 copy.88
  16.3 9.2 copy.41
  25.5 10.0 copy.27
  35.5 100.9 %all_to_all.21 = f32[16,128,1024]{1,2,0:T(8,128)} all-to-all(f32[16,128,1024]{1,2,0:T(8,128)} %bitcast.143), channel_id=1, replica_groups=mesh['row'=8,'col'=16] {'col'}, dimensions={0} | all-to-all | bytes 16777216 | tf_op jit(solution)/shard_map/all_to_all | solution.py:59
  136.5 9.2 copy.28
  145.7 10.8 copy.29
  156.5 7.2 all-to-all-start.1
  163.9 94.4 %all-to-all-done.1 = f32[1,2048,1024]{2,0,1:T(1,128)} async-done(((f32[1,2048,1024]{2,0,1:T(1,128)}), f32[1,2048,1024]{2,0,1:T(1,128)}, u32[]{:S(2)}, u32[]{:S(2)}) %all-to-all-start.1) | async-done | bytes 8388640 | tf_op jit(solution)/shard_map/all_to_all | solution.py:60
  258.3 4.4 constant_dynamic-slice_fusion.2
  262.7 4.6 copy.40
  273.2 145.4 %all-reduce.10.cloned.1.call-done = f32[512,512]{0,1:T(8,128)} async-done(((f32[512,512]{0,1:T(8,128)}), f32[512,512]{0,1:T(8,128)}) %all-reduce.10.cloned.1.call-update) | async-done | bytes 1048592 | tf_op jit(solution)/shard_map/psum | solution.py:71
  421.6 11.7 cholesky.85
  433.5 9.8 custom-call.34
  444.0 11.7 cholesky.180
  455.7 10.2 custom-call.35
  466.6 11.7 cholesky.201
  478.3 9.8 custom-call.36
  488.7 11.7 cholesky.218
  505.3 10.4 while.1
  515.7 40.1 %custom-call.37 = f32[4,128,128]{1,2,0:T(8,128)S(1)} custom-call(f32[4,128,128]{2,1,0:T(8,128)} %get-tuple-element.10), custom_call_target="InvertDiagBlocksLowerTriangular" | custom-call | tf_op jit(solution)/shard_map/jit(_solve_triangular)/triangular_solve | solution.py:13
  573.1 4.4 pad_maximum_fusion
  577.4 6.6 reshape.97
  586.5 8.8 fusion.9
  600.7 6.1 copy.43
  608.1 119.9 %all-reduce.16.cloned.1.call-done = f32[512,128]{1,0:T(8,128)} async-done(((f32[512,128]{1,0:T(8,128)}), f32[512,128]{1,0:T(8,128)}) %all-reduce.16.cloned.1.call-update) | async-done | bytes 262160 | tf_op jit(solution)/shard_map/psum | solution.py:121
  731.4 102.9 %all-reduce.14.cloned.1.call-done = f32[1024,512]{0,1:T(8,128)} async-done(((f32[1024,512]{0,1:T(8,128)}), f32[1024,512]{0,1:T(8,128)}) %all-reduce.14.cloned.1.call-update) | async-done | bytes 2097168 | tf_op jit(solution)/shard_map/psum | solution.py:9
  834.3 20.1 %bitcast_subtract_fusion = f32[2048,1024]{1,0:T(8,128)S(1)} fusion(f32[1,2048,1024]{2,0,1:T(1,128)} %all-to-all-done.1, f32[1024,512]{0,1:T(8,128)} %all-reduce.14.cloned.1.call-done, f32[128,2048]{1,0:T(8,128)} %copy-done.2, f32[128,2048]{1,0:T(8,128)} %copy-done.1, f32[128,2048]{1,0:T(8,128)S(1)} %fusion.83, f32[128,2048]{1,0:T(8,128)S(1)} %fusion.23), kind=kOutput, calls=%fused_computation.2 | convolution fusion | flops 12890144768 | bytes 23068672 | tf_op jit(solution)/shard_map/dot_general | solution.py:85
  860.7 141.0 %all-reduce.18.cloned.1.call-done = f32[512,128]{1,0:T(8,128)} async-done(((f32[512,128]{1,0:T(8,128)}), f32[512,128]{1,0:T(8,128)}) %all-reduce.18.cloned.1.call-update) | async-done | bytes 262160 | tf_op jit(solution)/shard_map/psum | solution.py:121
  1009.7 139.1 %all-reduce.20.cloned.1.call-done = f32[512,128]{1,0:T(8,128)} async-done(((f32[512,128]{1,0:T(8,128)}), f32[512,128]{1,0:T(8,128)}) %all-reduce.20.cloned.1.call-update) | async-done | bytes 262160 | tf_op jit(solution)/shard_map/psum | solution.py:121
  1156.5 139.3 %all-reduce.22.cloned.1.call-done = f32[512,128]{1,0:T(8,128)} async-done(((f32[512,128]{1,0:T(8,128)}), f32[512,128]{1,0:T(8,128)}) %all-reduce.22.cloned.1.call-update) | async-done | bytes 262160 | tf_op jit(solution)/shard_map/psum | solution.py:121
  1305.8 13.5 reshape.120
  1319.3 123.6 %all-reduce.24.cloned.1.call-done = f32[512,128]{1,0:T(8,128)} async-done(((f32[512,128]{1,0:T(8,128)}), f32[512,128]{1,0:T(8,128)}) %all-reduce.24.cloned.1.call-update) | async-done | bytes 262160 | tf_op jit(solution)/shard_map/psum | solution.py:121
  (133 shorter events, 92.5 us)
Async XLA Ops:
  7.2 7.6 copy-start.8
  156.5 101.7 %all-to-all-start.1 = ((f32[1,2048,1024]{2,0,1:T(1,128)}), f32[1,2048,1024]{2,0,1:T(1,128)}, u32[]{:S(2)}, u32[]{:S(2)}) async-start(f32[1,2048,1024]{2,0,1:T(1,128)} %copy.29), calls=%async_computation.1 | async-start | bytes 16777216 | tf_op jit(solution)/shard_map/all_to_all | solution.py:60
  163.7 254.8 %all-reduce.10.cloned.1.call-start = ((), (), s32[]{:S(2)}) async-start(), calls=%async_computation.2 | async-start | bytes 2097152 | tf_op jit(solution)/shard_map/psum | solution.py:71
  272.2 289.7 %all-reduce.12.cloned.1.call-start = ((), (), s32[]{:S(2)}) async-start(), calls=%async_computation.3 | async-start | bytes 8388608 | tf_op jit(solution)/shard_map/psum | solution.py:73
  272.9 455.0 %all-reduce.16.cloned.1.call-start = ((), (), s32[]{:S(2)}) async-start(), calls=%async_computation.5 | async-start | bytes 524288 | tf_op jit(solution)/shard_map/psum | solution.py:121
  559.7 1.5 copy-start.4
  561.2 0.6 copy-start.6
  561.9 5.7 copy-start.3
  569.9 7.5 copy-start.1
  573.0 4.4 copy-start.2
  586.1 248.2 %all-reduce.14.cloned.1.call-start = ((), (), s32[]{:S(2)}) async-start(), calls=%async_computation.4 | async-start | bytes 4194304 | tf_op jit(solution)/shard_map/psum | solution.py:9
  595.3 2.5 copy-start.5
  595.4 2.6 copy-start.7
  597.2 404.5 %all-reduce.18.cloned.1.call-start = ((), (), s32[]{:S(2)}) async-start(), calls=%async_computation.6 | async-start | bytes 524288 | tf_op jit(solution)/shard_map/psum | solution.py:121
  854.4 3.2 copy-start
  859.4 289.4 %all-reduce.20.cloned.1.call-start = ((), (), s32[]{:S(2)}) async-start(), calls=%async_computation.7 | async-start | bytes 524288 | tf_op jit(solution)/shard_map/psum | solution.py:121
  1008.1 287.7 %all-reduce.22.cloned.1.call-start = ((), (), s32[]{:S(2)}) async-start(), calls=%async_computation.8 | async-start | bytes 524288 | tf_op jit(solution)/shard_map/psum | solution.py:121
  1155.2 287.8 %all-reduce.24.cloned.1.call-start = ((), (), s32[]{:S(2)}) async-start(), calls=%async_computation.9 | async-start | bytes 524288 | tf_op jit(solution)/shard_map/psum | solution.py:121
Sparse Core Ops, SparseCore 0:
  272.3 146.2 all-reduce.9
  421.7 128.5 all-reduce.11
  586.2 141.7 all-reduce.15
  730.3 103.9 all-reduce.13
  859.5 142.1 all-reduce.17
  1008.2 140.4 all-reduce.19
  1155.3 140.4 all-reduce.21
  1302.3 140.5 all-reduce.23
where the time goes:
time: 1460 us
  waiting for transfers between devices  1010 us (69%)
  other arithmetic  136 us (9%)
  local copies, waits for them, and re-layouts  118 us (8%)
  blocking collectives  101 us (7%)
  matrix products  69.3 us (5%)
  between operations  18.1 us (1%)
    psum x5, waiting for transfers between devices, body(): lax.psum(place(partial_value, block_place, panel_width, 0), ('row', 'col'))  663 us
    psum x1, waiting for transfers between devices, body(): lax.psum(place(corner_piece, row_place, panel_width, 0), ('row', 'col'))  145 us
    psum x1, waiting for transfers between devices, spread_2(): return lax.psum(block, axis)  103 us
    all_to_all x1, blocking collectives, body(): lax.all_to_all(arranged, 'col', split_axis=0, concat_axis=1, tiled=True)  101 us
    all_to_all x1, waiting for transfers between devices, body(): lax.all_to_all(spread, 'row', split_axis=1, concat_axis=0, tiled=True)  94.4 us
    another operation x14, other arithmetic, body(): corner_factor = jnp.linalg.cholesky(corner)  78.7 us
    another operation x4, other arithmetic, right_solve(): jax.scipy.linalg.solve_triangular(corner_factor, panel_rows.T, lower=True)  44.6 us
    unnamed x28, local copies, waits for them, and re-layouts  38.7 us
  transfers between devices with their start and end apart: 9, of which 8 were waited for; matrix products, arithmetic and copies ran while one was open for 13% of the time, Pallas kernels for 0%

commit v1 on v0

--- a/solution.py
+++ b/solution.py
@@ -4,9 +4,15 @@
 from jax.sharding import PartitionSpec as P
 
 
+def gather_and_add(x, axis):
+    parts = lax.all_gather(x, axis, axis=0, tiled=False)
+    total = parts.sum(axis=0)
+    return total
+
+
 def spread_2(block, axis, source):
     block = jnp.where(lax.axis_index(axis) == source, block, jnp.zeros_like(block))
-    return lax.psum(block, axis)
+    return gather_and_add(block, axis)
 
 
 def right_solve(corner_factor, panel_rows):

time: 1460 us -> 1560 us (1.068)
  waiting for transfers between devices: 1010 us -> 1080 us
    all_gather x0 -> x1, waiting for transfers between devices: none -> 178 us  [gather_and_add(): parts = lax.all_gather(x, axis, axis=0, tiled=False)]
    psum x1 -> x0, waiting for transfers between devices: 103 us -> none  [spread_2(): return lax.psum(block, axis)]
    unnamed x28 -> x27, local copies, waits for them, and re-layouts: 38.7 us -> 36.9 us
  transfers between devices with their start and end apart: 9 -> 9, of which waited for: 8 -> 8; matrix products, arithmetic and copies ran while one was open for 13% -> 12% of each run, Pallas kernels for 0% -> 0%
where the time goes in v1:
time: 1560 us; the launch traced here: 1550 us
  waiting for transfers between devices  1080 us (69%)
  other arithmetic  142 us (9%)
  local copies, waits for them, and re-layouts  123 us (8%)
  blocking collectives  101 us (6%)
  matrix products  81.6 us (5%)
  between operations  18.2 us (1%)
    psum x5, waiting for transfers between devices, body(): lax.psum(place(partial_value, block_place, panel_width, 0), ('row', 'col'))  661 us
    all_gather x1, waiting for transfers between devices, gather_and_add(): parts = lax.all_gather(x, axis, axis=0, tiled=False)  178 us
    psum x1, waiting for transfers between devices, body(): lax.psum(place(corner_piece, row_place, panel_width, 0), ('row', 'col'))  145 us
    all_to_all x1, blocking collectives, body(): lax.all_to_all(arranged, 'col', split_axis=0, concat_axis=1, tiled=True)  101 us
    all_to_all x1, waiting for transfers between devices, body(): lax.all_to_all(spread, 'row', split_axis=1, concat_axis=0, tiled=True)  94.4 us
    another operation x14, other arithmetic, body(): corner_factor = jnp.linalg.cholesky(corner)  78.8 us
    another operation x4, other arithmetic, right_solve(): jax.scipy.linalg.solve_triangular(corner_factor, panel_rows.T, lower=True)  44.6 us
    unnamed x27, local copies, waits for them, and re-layouts  36.9 us
  transfers between devices with their start and end apart: 9, of which 8 were waited for; matrix products, arithmetic and copies ran while one was open for 12% of the time, Pallas kernels for 0%

profile of v1, /device:TPU:1, one launch (start us, length us, event | category | flops | bytes accessed | tf_op | source)
XLA Modules:
  0.0 1553.3 jit_solution(16054793109916458360)
XLA Ops:
  7.2 7.6 copy.92
  16.3 9.2 copy.46
  25.5 10.0 copy.29
  35.5 100.9 %all_to_all.21 = f32[16,128,1024]{1,2,0:T(8,128)} all-to-all(f32[16,128,1024]{1,2,0:T(8,128)} %bitcast.140), channel_id=1, replica_groups=mesh['row'=8,'col'=16] {'col'}, dimensions={0} | all-to-all | bytes 16777216 | tf_op jit(solution)/shard_map/all_to_all | solution.py:65
  136.5 9.2 copy.30
  145.7 10.9 copy.31
  156.6 7.2 all-to-all-start.1
  163.9 94.4 %all-to-all-done.1 = f32[1,2048,1024]{2,0,1:T(1,128)} async-done(((f32[1,2048,1024]{2,0,1:T(1,128)}), f32[1,2048,1024]{2,0,1:T(1,128)}, u32[]{:S(2)}, u32[]{:S(2)}) %all-to-all-start.1) | async-done | bytes 8388640 | tf_op jit(solution)/shard_map/all_to_all | solution.py:66
  262.7 4.6 copy.45
  273.2 145.4 %all-reduce.9.cloned.1.call-done = f32[512,512]{0,1:T(8,128)} async-done(((f32[512,512]{0,1:T(8,128)}), f32[512,512]{0,1:T(8,128)}) %all-reduce.9.cloned.1.call-update) | async-done | bytes 1048592 | tf_op jit(solution)/shard_map/psum | solution.py:77
  421.6 11.7 cholesky.85
  433.5 9.8 custom-call.34
  444.0 11.7 cholesky.180
  455.7 10.2 custom-call.35
  466.6 11.7 cholesky.201
  478.4 9.8 custom-call.36
  488.8 11.7 cholesky.218
  505.5 10.9 while.1
  516.4 40.1 %custom-call.37 = f32[4,128,128]{1,2,0:T(8,128)S(1)} custom-call(f32[4,128,128]{2,1,0:T(8,128)} %get-tuple-element.10), custom_call_target="InvertDiagBlocksLowerTriangular" | custom-call | tf_op jit(solution)/shard_map/jit(_solve_triangular)/triangular_solve | solution.py:19
  578.2 6.6 reshape.107
  587.3 5.7 broadcast_select_fusion
  593.0 6.1 copy.34
  602.5 6.1 copy.47
  609.9 118.7 %all-reduce.13.cloned.1.call-done = f32[512,128]{1,0:T(8,128)} async-done(((f32[512,128]{1,0:T(8,128)}), f32[512,128]{1,0:T(8,128)}) %all-reduce.13.cloned.1.call-update) | async-done | bytes 262160 | tf_op jit(solution)/shard_map/psum | solution.py:127
  732.1 177.9 %all-gather.2.cloned.1.call-done = f32[8,1024,512]{2,1,0:T(8,128)} async-done(((f32[1,1024,512]{2,1,0:T(8,128)}), f32[8,1024,512]{2,1,0:T(8,128)}) %all-gather.2.cloned.1.call-update) | async-done | bytes 16777232 | tf_op jit(solution)/shard_map/all_gather | solution.py:8
  909.9 9.4 reduce_sum.9
  919.3 32.4 %bitcast_subtract_fusion = f32[2048,1024]{1,0:T(8,128)S(1)} fusion(f32[1,2048,1024]{2,0,1:T(1,128)} %all-to-all-done.1, f32[1024,512]{1,0:T(8,128)} %reduce_sum.9, f32[128,2048]{1,0:T(8,128)} %copy-done.2, f32[128,2048]{1,0:T(8,128)} %copy-done.1, f32[128,2048]{1,0:T(8,128)S(1)} %fusion.82, f32[128,2048]{1,0:T(8,128)S(1)} %fusion.22), kind=kOutput, calls=%fused_computation.2 | convolution fusion | flops 12890144768 | bytes 23068672 | tf_op jit(solution)/shard_map/dot_general | solution.py:91
  958.0 140.4 %all-reduce.15.cloned.1.call-done = f32[512,128]{1,0:T(8,128)} async-done(((f32[512,128]{1,0:T(8,128)}), f32[512,128]{1,0:T(8,128)}) %all-reduce.15.cloned.1.call-update) | async-done | bytes 262160 | tf_op jit(solution)/shard_map/psum | solution.py:127
  1106.2 139.3 %all-reduce.17.cloned.1.call-done = f32[512,128]{1,0:T(8,128)} async-done(((f32[512,128]{1,0:T(8,128)}), f32[512,128]{1,0:T(8,128)}) %all-reduce.17.cloned.1.call-update) | async-done | bytes 262160 | tf_op jit(solution)/shard_map/psum | solution.py:127
  1253.2 139.4 %all-reduce.19.cloned.1.call-done = f32[512,128]{1,0:T(8,128)} async-done(((f32[512,128]{1,0:T(8,128)}), f32[512,128]{1,0:T(8,128)}) %all-reduce.19.cloned.1.call-update) | async-done | bytes 262160 | tf_op jit(solution)/shard_map/psum | solution.py:127
  1402.6 13.7 reshape.130
  1416.4 123.4 %all-reduce.21.cloned.1.call-done = f32[512,128]{1,0:T(8,128)} async-done(((f32[512,128]{1,0:T(8,128)}), f32[512,128]{1,0:T(8,128)}) %all-reduce.21.cloned.1.call-update) | async-done | bytes 262160 | tf_op jit(solution)/shard_map/psum | solution.py:127
  (134 shorter events, 99.9 us)
Async XLA Ops:
  7.2 7.6 copy-start.8
  156.6 101.7 %all-to-all-start.1 = ((f32[1,2048,1024]{2,0,1:T(1,128)}), f32[1,2048,1024]{2,0,1:T(1,128)}, u32[]{:S(2)}, u32[]{:S(2)}) async-start(f32[1,2048,1024]{2,0,1:T(1,128)} %copy.31), calls=%async_computation.1 | async-start | bytes 16777216 | tf_op jit(solution)/shard_map/all_to_all | solution.py:66
  163.8 254.8 %all-reduce.9.cloned.1.call-start = ((), (), s32[]{:S(2)}) async-start(), calls=%async_computation.2 | async-start | bytes 2097152 | tf_op jit(solution)/shard_map/psum | solution.py:77
  272.2 290.4 %all-reduce.11.cloned.1.call-start = ((), (), s32[]{:S(2)}) async-start(), calls=%async_computation.3 | async-start | bytes 8388608 | tf_op jit(solution)/shard_map/psum | solution.py:79
  273.0 455.7 %all-reduce.13.cloned.1.call-start = ((), (), s32[]{:S(2)}) async-start(), calls=%async_computation.5 | async-start | bytes 524288 | tf_op jit(solution)/shard_map/psum | solution.py:127
  560.4 1.5 copy-start.4
  561.9 0.6 copy-start.6
  562.6 5.7 copy-start.3
  570.6 7.5 copy-start.1
  573.7 4.4 copy-start.2
  586.8 323.1 %all-gather.2.cloned.1.call-start = ((), (), s32[]{:S(2)}) async-start(), calls=%async_computation.4 | async-start | bytes 18874368 | tf_op jit(solution)/shard_map/all_gather | solution.py:8
  593.0 6.8 copy-start.5
  593.0 6.9 copy-start.7
  599.1 499.3 %all-reduce.15.cloned.1.call-start = ((), (), s32[]{:S(2)}) async-start(), calls=%async_computation.6 | async-start | bytes 524288 | tf_op jit(solution)/shard_map/psum | solution.py:127
  951.7 3.2 copy-start
  956.7 288.8 %all-reduce.17.cloned.1.call-start = ((), (), s32[]{:S(2)}) async-start(), calls=%async_computation.7 | async-start | bytes 524288 | tf_op jit(solution)/shard_map/psum | solution.py:127
  1104.8 287.8 %all-reduce.19.cloned.1.call-start = ((), (), s32[]{:S(2)}) async-start(), calls=%async_computation.8 | async-start | bytes 524288 | tf_op jit(solution)/shard_map/psum | solution.py:127
  1251.9 287.9 %all-reduce.21.cloned.1.call-start = ((), (), s32[]{:S(2)}) async-start(), calls=%async_computation.9 | async-start | bytes 524288 | tf_op jit(solution)/shard_map/psum | solution.py:127
Sparse Core Ops, SparseCore 0:
  272.3 146.2 all-reduce.8
  421.7 128.4 all-reduce.10
  586.9 141.6 all-reduce.12
  730.8 179.0 all-gather.1
  956.8 141.5 all-reduce.14
  1105.0 140.4 all-reduce.16
  1252.0 140.5 all-reduce.18
  1399.2 140.5 all-reduce.20
